TPU v7x, 512 devices: a whole 4x8x8 slice. The times are simulated.
512 devices in a mesh: req: 32 (over z_hi, x, core), seq: 16 (over z_lo, y).
Axes of the slice: x: 4, y: 8, z: 8 (z_hi: 4, z_lo: 2; z = z_hi * 2 + z_lo), core: 2. Of those that a mesh axis runs over, the one named last changes fastest.
Arguments:
- layer_input: bfloat16 [32, 256, 2048], P('req', 'seq'), may hold values from -3 to 3
- queries: bfloat16 [32, 256, 4096], P('req', 'seq'), may hold values from -4.5 to 4.5
- fresh_kv: bfloat16 [32, 256, 1024], P('req', 'seq'), may hold values from -4.5 to 4.5
- cache_kv: bfloat16 [32, 1792, 1024], P('req', 'seq'), may hold values from -4.5 to 4.5
- cached_len: int32 [32], P('req'), may hold values from 2 to 1792, as said below
- out_weight: bfloat16 [4096, 2048], P('seq', 'req'), may hold values from -0.09375 to 0.09375
- norm_gain: float32 [2048], replicated, may hold values from 0.5 to 1.5
- routes: int32 [32, 256, 8], P('req', 'seq'), may hold values from 0 to 127, all different within a row; in each aligned block of 16 rows (0 to 15, 16 to 31, ..., all dimensions but the last counted through in order) at most 2 rows name the same one
- route_gates: float32 [32, 256, 8], P('req', 'seq'), may hold values from 0.2 to 1
- w_gate_up: bfloat16 [512, 2048, 384], P(('req', 'seq')), may hold values from -0.125 to 0.125
- w_down: bfloat16 [512, 192, 2048], P(('req', 'seq')), may hold values from -0.21875 to 0.21875
Outputs:
- output: bfloat16 [32, 256, 2048], P('req', 'seq')
Inputs may be any that keep to these rules, and one draw needn't show every extreme that they name: Request r has cached_len[r] valid cached rows; some request has exactly 1792. `routes`: each token names 8 different experts; among the 16 tokens of one device (aligned blocks), no expert is named more than 2 times.
All inputs are finite; a program needn't handle non-finite values.
Results may differ from a plain program's by a relative error of at most 0.03.
Values may be sent and summed in bfloat16 or wider, within the bound.
A program may use at most 64 MiB of HBM per device.

v0:
```python
import math
import jax
import jax.numpy as jnp
from jax import lax
from jax.sharding import PartitionSpec as P

QH = 32
KVH = 4
HD = 128
EXPERTS = 128
TOP = 8
CAP = 2
neg_large = -1e30
epsilon = 1e-06


def local(
    layer_input,
    queries,
    fresh_kv,
    cache_kv,
    cached_len,
    out_weight,
    norm_gain,
    routes,
    route_gates,
    w_gate_up,
    w_down,
):
    new_dev = queries.shape[1]
    cache_dev = cache_kv.shape[1]
    query_width = queries.shape[2]
    kv_width = fresh_kv.shape[2] // 2
    seq_count = lax.axis_size("seq")
    req_count = lax.axis_size("req")
    group_size = QH // KVH
    scale = 1.0 / math.sqrt(HD)
    block_rows = cache_dev + new_dev
    length = cached_len[0]
    query_pos = lax.axis_index("seq") * new_dev + jnp.arange(new_dev, dtype=jnp.int32)
    grouped = queries[0].reshape(new_dev, KVH, group_size, HD)
    key_block = jnp.concatenate([cache_kv[0], fresh_kv[0]], 0)
    shard_rows = lax.all_gather(key_block, "seq", axis=0, tiled=True)
    row_count = shard_rows.shape[0]
    row_index = jnp.arange(row_count, dtype=jnp.int32)
    source_dev = row_index // block_rows
    within = row_index % block_rows
    in_cache = within < cache_dev
    cache_live = source_dev * cache_dev + within < length
    fresh_live = (source_dev * new_dev + within - cache_dev)[None, :] <= query_pos[:, None]
    visible = jnp.where(in_cache[None, :], cache_live[None, :], fresh_live)
    running_max = jnp.full((new_dev, KVH, group_size), neg_large, jnp.float32)
    key_part = shard_rows[:, :kv_width].reshape(row_count, KVH, HD)
    value_part = shard_rows[:, kv_width:].reshape(row_count, KVH, HD)
    scores = (
        jnp.einsum("ngqc,pgc->ngqp", grouped, key_part, preferred_element_type=jnp.float32) * scale
    )
    mask = visible[:, None, None, :]
    scores = jnp.where(mask, scores, neg_large)
    new_max = jnp.maximum(running_max, jnp.max(scores, axis=-1))
    weights = jnp.where(mask, jnp.exp(scores - new_max[..., None]), 0.0)
    denominator = jnp.sum(weights, axis=-1)
    mixed_values = jnp.einsum(
        "ngqp,pgc->ngqc",
        weights.astype(jnp.bfloat16),
        value_part,
        preferred_element_type=jnp.float32,
    )
    numerator = mixed_values
    running_max, denominator, numerator = (new_max, denominator, numerator)
    attended = (
        (numerator / denominator[..., None]).reshape(new_dev, query_width).astype(jnp.bfloat16)
    )
    by_heads = lax.all_to_all(attended, "seq", split_axis=1, concat_axis=0, tiled=True)
    proj_full = lax.all_gather(out_weight, "req", axis=1, tiled=True)
    projected = lax.psum_scatter(
        jnp.dot(by_heads, proj_full, preferred_element_type=jnp.float32).astype(jnp.bfloat16),
        "seq",
        scatter_dimension=0,
        tiled=True,
    ).astype(jnp.float32)
    residual = (layer_input[0].astype(jnp.float32) + projected).astype(jnp.bfloat16)
    residual_f = residual.astype(jnp.float32)
    normed = (
        residual_f
        * lax.rsqrt(jnp.mean(residual_f * residual_f, axis=-1, keepdims=True) + epsilon)
        * norm_gain
    ).astype(jnp.bfloat16)
    owned_count = EXPERTS // req_count
    slab_count = w_gate_up.shape[0]
    split_count = seq_count * slab_count // owned_count
    hidden_part = w_down.shape[1]
    model_width = normed.shape[1]
    pair_count = new_dev * TOP
    chosen = routes[0].reshape(pair_count)
    onehot = (chosen[:, None] == jnp.arange(EXPERTS, dtype=jnp.int32)[None, :]).astype(jnp.int32)
    earlier = jnp.cumsum(onehot, axis=0) - onehot
    slot_at = jnp.sum(earlier * onehot, axis=1)
    target = chosen * CAP + slot_at
    placed = (target[:, None] == jnp.arange(EXPERTS * CAP, dtype=jnp.int32)[None, :]).astype(
        jnp.float32
    )
    placed_rows = placed.reshape(new_dev, TOP, EXPERTS * CAP)
    picker = jnp.sum(placed_rows, axis=1).astype(jnp.bfloat16)
    outgoing = lax.dot_general(
        picker, normed, (((0,), (0,)), ((), ())), preferred_element_type=jnp.float32
    )
    outgoing = outgoing.astype(jnp.bfloat16).reshape(req_count, owned_count, CAP, model_width)
    combine_rows = jnp.sum(placed_rows * route_gates[0][:, :, None], axis=1)
    arrived_req = lax.all_to_all(outgoing, "req", split_axis=0, concat_axis=0, tiled=True)
    spread_out = jnp.broadcast_to(
        arrived_req[:, :, None], (req_count, owned_count, split_count, CAP, model_width)
    )
    arrived = lax.all_to_all(
        spread_out.reshape(req_count, seq_count, slab_count, CAP, model_width),
        "seq",
        split_axis=1,
        concat_axis=1,
        tiled=True,
    )
    token_rows = arrived[:, :, 0].reshape(req_count * seq_count * CAP, model_width)
    both = jnp.dot(token_rows, w_gate_up[0], preferred_element_type=jnp.float32)
    hidden = (jax.nn.silu(both[:, :hidden_part]) * both[:, hidden_part:]).astype(jnp.bfloat16)
    part_out = jnp.dot(hidden, w_down[0], preferred_element_type=jnp.float32).astype(jnp.bfloat16)
    produced_list = [part_out.reshape(req_count, seq_count, CAP, model_width)]
    produced = jnp.stack(produced_list, axis=2)
    returned = lax.all_to_all(produced, "seq", split_axis=1, concat_axis=1, tiled=True)
    grouped_parts = returned.reshape(req_count, owned_count, split_count, CAP, model_width).astype(
        jnp.float32
    )
    result = lax.all_to_all(
        jnp.sum(grouped_parts, axis=2).astype(jnp.bfloat16),
        "req",
        split_axis=0,
        concat_axis=0,
        tiled=True,
    )
    expert_rows = result.reshape(EXPERTS * CAP, model_width).astype(jnp.float32)
    mixture = jnp.dot(combine_rows, expert_rows, precision=lax.Precision.HIGHEST)
    output = (residual_f + mixture).astype(jnp.bfloat16)
    return output[None]


def solution(mesh):
    return jax.shard_map(
        local,
        mesh=mesh,
        in_specs=(
            P("req", "seq", None),
            P("req", "seq", None),
            P("req", "seq", None),
            P("req", "seq", None),
            P("req"),
            P("seq", "req"),
            P(),
            P("req", "seq", None),
            P("req", "seq", None),
            P(("req", "seq"), None, None),
            P(("req", "seq"), None, None),
        ),
        out_specs=P("req", "seq", None),
        check_vma=False,
    )
```

profile of v0, /device:TPU:12, one launch (start us, length us, event | category | flops | bytes accessed | tf_op | source)
XLA Modules:
  0.0 570.8 jit_solution(9128146810409177649)
XLA Ops:
  6.5 1.2 copy.99
  7.8 0.9 copy.100
  8.7 0.9 pad_maximum_fusion
  11.0 0.9 copy.120
  12.1 91.9 %all-gather.3.cloned.1.call-done = bf16[2048,1024]{0,1:T(8,128)(2,1)} async-done(((bf16[128,1024]{0,1:T(8,128)(2,1)}), bf16[2048,1024]{0,1:T(8,128)(2,1)}) %all-gather.3.cloned.1.call-update) | async-done | bytes 4194320 | tf_op jit(solution)/shard_map/all_gather | solution.py:43
  103.9 2.8 fusion.51
  106.7 1.0 fusion
  107.7 1.2 fusion.1
  108.9 1.1 fusion.16
  110.8 7.8 %all-to-all-start = ((bf16[16,16,256]{2,0,1:T(8,128)(2,1)}), bf16[16,16,256]{2,0,1:T(8,128)(2,1)S(1)}, u32[]{:S(2)}, u32[]{:S(2)}) async-start(bf16[16,16,256]{2,0,1:T(8,128)(2,1)} %copy.105), calls=%async_computation | async-start | bytes 262144 | tf_op jit(solution)/shard_map/all_to_all | solution.py:74
  118.7 46.1 %all-gather.5.cloned.1.call-done = bf16[256,2048]{0,1:T(8,128)(2,1)} async-done(((bf16[256,64]{0,1:T(8,128)(2,1)}), bf16[256,2048]{0,1:T(8,128)(2,1)}) %all-gather.5.cloned.1.call-update) | async-done | bytes 1048592 | tf_op jit(solution)/shard_map/all_gather | solution.py:75
  164.8 2.7 convolution_convert_fusion.1
  168.6 69.4 %reduce-scatter.2.cloned.1.call-done = bf16[16,2048]{1,0:T(8,128)(2,1)} async-done(((bf16[256,2048]{1,0:T(8,128)(2,1)}), bf16[16,2048]{1,0:T(8,128)(2,1)}) %reduce-scatter.2.cloned.1.call-update) | async-done | bytes 65552 | tf_op jit(solution)/shard_map/reduce_scatter | solution.py:76
  238.0 1.0 fusion.23
  239.0 1.3 convolution_convert_fusion.2
  240.3 1.5 reshape.147
  241.9 38.3 %all_to_all.36 = bf16[32,4,2,2048]{3,2,1,0:T(2,128)(2,1)S(1)} all-to-all(bf16[32,4,2,2048]{3,2,1,0:T(2,128)(2,1)} %reshape.147), channel_id=1, replica_groups=mesh['req'=32,'seq'=16] {'req'}, dimensions={0} | all-to-all | bytes 2097152 | tf_op jit(solution)/shard_map/all_to_all | solution.py:110
  280.2 0.8 copy.110
  281.0 5.4 broadcast_in_dim.64
  286.4 98.3 %all_to_all.37 = bf16[32,16,1,2,2048]{4,3,0,2,1:T(2,128)(2,1)S(1)} all-to-all(bf16[32,16,1,2,2048]{4,3,0,2,1:T(2,128)(2,1)} %bitcast.81), channel_id=1, replica_groups=mesh['req'=32,'seq'=16] {'seq'}, dimensions={1} | all-to-all | bytes 8388608 | tf_op jit(solution)/shard_map/all_to_all | solution.py:114
  384.8 6.5 %copy.111 = bf16[32,16,1,2,2048]{4,3,1,0,2:T(2,128)(2,1)} copy(bf16[32,16,1,2,2048]{4,3,0,2,1:T(2,128)(2,1)S(1)} %all_to_all.37) | data formatting | bytes 8388608 | tf_op jit(solution)/shard_map/all_to_all | solution.py:114
  391.2 7.2 %reshape_squeeze.8 = bf16[1024,2048]{1,0:T(8,128)(2,1)} reshape(bf16[32,16,1,2,2048]{4,3,1,0,2:T(2,128)(2,1)} %copy.111) | data formatting | bytes 8388608 | tf_op jit(solution)/shard_map/reshape;squeeze | solution.py:121
  398.4 4.1 fusion.8
  402.5 3.2 convolution_convert_fusion
  405.8 7.6 %stack_reshape.3 = bf16[32,16,1,2,2048]{4,3,1,0,2:T(2,128)(2,1)} reshape(bf16[1024,2048]{1,0:T(8,128)(2,1)} %convolution_convert_fusion) | data formatting | bytes 8388608 | tf_op jit(solution)/shard_map/stack;reshape | solution.py:126
  413.4 6.0 %copy.112 = bf16[32,16,1,2,2048]{4,3,0,2,1:T(2,128)(2,1)S(1)} copy(bf16[32,16,1,2,2048]{4,3,1,0,2:T(2,128)(2,1)} %stack_reshape.3) | data formatting | bytes 8388608 | tf_op jit(solution)/shard_map/stack;reshape | solution.py:126
  419.5 97.5 %all_to_all.38 = bf16[32,16,1,2,2048]{4,3,0,2,1:T(2,128)(2,1)} all-to-all(bf16[32,16,1,2,2048]{4,3,0,2,1:T(2,128)(2,1)S(1)} %copy.112), channel_id=1, replica_groups=mesh['req'=32,'seq'=16] {'seq'}, dimensions={1} | all-to-all | bytes 8388608 | tf_op jit(solution)/shard_map/all_to_all | solution.py:127
  516.9 7.2 %bitcast_reduce_fusion = bf16[32,4,2,2048]{3,2,0,1:T(2,128)(2,1)S(1)} fusion(bf16[32,4,4,2,2048]{4,3,0,2,1:T(2,128)(2,1)} %bitcast.82), kind=kLoop, calls=%fused_computation | loop fusion | flops 1572864 | bytes 5242880 | tf_op jit(solution)/shard_map/reduce_sum | solution.py:132
  524.2 1.1 copy.113
  525.3 36.3 %all_to_all.39 = bf16[32,4,2,2048]{3,2,1,0:T(2,128)(2,1)} all-to-all(bf16[32,4,2,2048]{3,2,1,0:T(2,128)(2,1)S(1)} %copy.113), channel_id=1, replica_groups=mesh['req'=32,'seq'=16] {'req'}, dimensions={0} | all-to-all | bytes 2097152 | tf_op jit(solution)/shard_map/all_to_all | solution.py:131
  561.6 1.5 reshape.150
  563.1 1.2 fusion.4
  (41 shorter events, 2.8 us)
Async XLA Ops:
  6.5 391.9 %copy-start = (bf16[1,2048,384]{2,1,0:T(8,128)(2,1)S(1)}, bf16[1,2048,384]{2,1,0:T(8,128)(2,1)}, u32[]{:S(2)}) copy-start(bf16[1,2048,384]{2,1,0:T(8,128)(2,1)} %param.20) | copy-start | bytes 4718596
  6.5 97.4 %all-gather.3.cloned.1.call-start = ((), (), s32[]{:S(2)}) async-start(), calls=%async_computation.6 | async-start | bytes 4456448 | tf_op jit(solution)/shard_map/all_gather | solution.py:43
  9.6 155.2 %all-gather.5.cloned.1.call-start = ((), (), s32[]{:S(2)}) async-start(), calls=%async_computation.7 | async-start | bytes 1081344 | tf_op jit(solution)/shard_map/all_gather | solution.py:75
  110.0 57.5 %copy-start.3 = (s32[1,16,8]{1,2,0:T(8,128)S(1)}, s32[1,16,8]{1,2,0:T(8,128)}, u32[]{:S(2)}) copy-start(s32[1,16,8]{1,2,0:T(8,128)} %param.18) | copy-start | bytes 1540
  110.0 58.4 %copy-start.5 = (f32[1,16,8]{1,2,0:T(8,128)S(1)}, f32[1,16,8]{1,2,0:T(8,128)}, u32[]{:S(2)}) copy-start(f32[1,16,8]{1,2,0:T(8,128)} %param.19) | copy-start | bytes 1540
  110.0 128.0 %copy-start.1 = (bf16[1,16,2048]{2,1,0:T(8,128)(2,1)S(1)}, bf16[1,16,2048]{2,1,0:T(8,128)(2,1)}, u32[]{:S(2)}) copy-start(bf16[1,16,2048]{2,1,0:T(8,128)(2,1)} %param.11) | copy-start | bytes 196612
  110.0 129.0 %copy-start.4 = (f32[2048]{0:T(1024)S(1)}, f32[2048]{0:T(1024)}, u32[]{:S(2)}) copy-start(f32[2048]{0:T(1024)} %param.17) | copy-start | bytes 24580
  110.8 54.0 %all-to-all-start = ((bf16[16,16,256]{2,0,1:T(8,128)(2,1)}), bf16[16,16,256]{2,0,1:T(8,128)(2,1)S(1)}, u32[]{:S(2)}, u32[]{:S(2)}) async-start(bf16[16,16,256]{2,0,1:T(8,128)(2,1)} %copy.105), calls=%async_computation | async-start | bytes 262144 | tf_op jit(solution)/shard_map/all_to_all | solution.py:74
  118.6 119.4 %reduce-scatter.2.cloned.1.call-start = ((), (), s32[]{:S(2)}) async-start(), calls=%async_computation.8 | async-start | bytes 1114112 | tf_op jit(solution)/shard_map/reduce_scatter | solution.py:76
  398.4 4.1 copy-start.6
  524.2 39.0 %copy-start.2 = (bf16[16,2048]{1,0:T(8,128)(2,1)S(1)}, bf16[16,2048]{1,0:T(8,128)(2,1)}, u32[]{:S(2)}) copy-start(bf16[16,2048]{1,0:T(8,128)(2,1)} %reduce-scatter.2.cloned.1.call-done) | copy-start | bytes 196612
Sparse Core Ops, SparseCore 0:
  9.7 94.1 all-gather.2
  107.1 57.6 all-gather.4
  167.6 70.3 reduce-scatter.1
where the time goes:
time: 572 us; the launch traced here: 571 us
  blocking collectives  271 us (47%)
  waiting for transfers between devices  208 us (36%)
  local copies, waits for them, and re-layouts  44.8 us (8%)
  matrix products  14.5 us (3%)
  between operations  14 us (2%)
  other arithmetic  10.9 us (2%)
  starting transfers between devices  7.91 us (1%)
    all_to_all x1, blocking collectives, local(): lax.all_to_all(spread_out.reshape(req_count, seq_count, slab_count, CAP,...  98.3 us
    all_to_all x1, blocking collectives, local(): lax.all_to_all(produced, 'seq', split_axis=1, concat_axis=1, tiled=True)  97.5 us
    all_gather x1, waiting for transfers between devices, local(): shard_rows = lax.all_gather(key_block, 'seq', axis=0, tiled=True)  91.9 us
    reduce_scatter x1, waiting for transfers between devices, local(): lax.psum_scatter(jnp.dot(by_heads, proj_full, preferred_element_type=jnp....  69.4 us
    all_gather x1, waiting for transfers between devices, local(): proj_full = lax.all_gather(out_weight, 'req', axis=1, tiled=True)  46.1 us
    all_to_all x1, blocking collectives, local(): lax.all_to_all(outgoing, 'req', split_axis=0, concat_axis=0, tiled=True)  38.3 us
    all_to_all x1, blocking collectives, local(): lax.all_to_all(jnp.sum(grouped_parts, axis=2).astype(jnp.bfloat16), 'req'...  36.3 us
    another operation x2, local copies, waits for them, and re-layouts, local(): produced = jnp.stack(produced_list, axis=2)  13.7 us
  transfers between devices with their start and end apart: 4, of which 3 were waited for; matrix products, arithmetic and copies ran while one was open for 2% of the time, Pallas kernels for 0%

commit v1 on v0

--- a/solution.py
+++ b/solution.py
@@ -40,7 +40,9 @@
     query_pos = lax.axis_index("seq") * new_dev + jnp.arange(new_dev, dtype=jnp.int32)
     grouped = queries[0].reshape(new_dev, KVH, group_size, HD)
     key_block = jnp.concatenate([cache_kv[0], fresh_kv[0]], 0)
-    shard_rows = lax.all_gather(key_block, "seq", axis=0, tiled=True)
+    shard_rows = jnp.concatenate(
+        lax.all_to_all(jnp.stack([key_block] * lax.axis_size("seq")), "seq", 0, 0), axis=0
+    )
     row_count = shard_rows.shape[0]
     row_index = jnp.arange(row_count, dtype=jnp.int32)
     source_dev = row_index // block_rows

time: 572 us -> 548 us (0.958)
  waiting for transfers between devices: 208 us -> 173 us
  starting transfers between devices: 7.91 us -> 17.6 us
    all_to_all x0 -> x1, waiting for transfers between devices: none -> 94.4 us  [local(): lax.all_to_all(jnp.stack([key_block] * lax.axis_size('seq')), 'seq', 0, 0)]
    all_gather x1 -> x0, waiting for transfers between devices: 91.9 us -> none  [local(): shard_rows = lax.all_gather(key_block, 'seq', axis=0, tiled=True)]
    all_gather x1, waiting for transfers between devices: 46.1 us -> 0.02 us  [local(): proj_full = lax.all_gather(out_weight, 'req', axis=1, tiled=True)]
    all_to_all x0 -> x1, starting transfers between devices: none -> 9.5 us  [local(): lax.all_to_all(jnp.stack([key_block] * lax.axis_size('seq')), 'seq', 0, 0)]
    all_to_all x1, waiting for transfers between devices: 0.01 us -> 7.84 us  [local(): lax.all_to_all(attended, 'seq', split_axis=1, concat_axis=0, tiled=True)]
where the time goes in v1:
time: 548 us; the launch traced here: 547 us
  blocking collectives  271 us (49%)
  waiting for transfers between devices  173 us (32%)
  local copies, waits for them, and re-layouts  45.1 us (8%)
  starting transfers between devices  17.6 us (3%)
  matrix products  14.6 us (3%)
  between operations  14.3 us (3%)
  other arithmetic  11.2 us (2%)
    all_to_all x1, blocking collectives, local(): lax.all_to_all(spread_out.reshape(req_count, seq_count, slab_count, CAP,...  98.5 us
    all_to_all x1, blocking collectives, local(): lax.all_to_all(produced, 'seq', split_axis=1, concat_axis=1, tiled=True)  97.5 us
    all_to_all x1, waiting for transfers between devices, local(): lax.all_to_all(jnp.stack([key_block] * lax.axis_size('seq')), 'seq', 0, 0)  94.4 us
    reduce_scatter x1, waiting for transfers between devices, local(): lax.psum_scatter(jnp.dot(by_heads, proj_full, preferred_element_type=jnp....  70.4 us
    all_to_all x1, blocking collectives, local(): lax.all_to_all(outgoing, 'req', split_axis=0, concat_axis=0, tiled=True)  38.2 us
    all_to_all x1, blocking collectives, local(): lax.all_to_all(jnp.sum(grouped_parts, axis=2).astype(jnp.bfloat16), 'req'...  36.4 us
    another operation x2, local copies, waits for them, and re-layouts, local(): produced = jnp.stack(produced_list, axis=2)  13.7 us
  transfers between devices with their start and end apart: 4, of which 3 were waited for; matrix products, arithmetic and copies ran while one was open for 2% of the time, Pallas kernels for 0%

profile of v1, /device:TPU:12, one launch (start us, length us, event | category | flops | bytes accessed | tf_op | source)
XLA Modules:
  0.0 546.7 jit_solution(10823000766652491730)
XLA Ops:
  6.5 1.1 pad_maximum_fusion
  7.8 2.8 stack.2
  10.6 9.5 %all-to-all-start = ((bf16[16,128,1024]{1,2,0:T(8,128)(2,1)}), bf16[16,128,1024]{1,2,0:T(8,128)(2,1)}, u32[]{:S(2)}, u32[]{:S(2)}) async-start(bf16[16,128,1024]{1,2,0:T(8,128)(2,1)} %stack.2), calls=%async_computation | async-start | bytes 8388608 | tf_op jit(solution)/shard_map/all_to_all | solution.py:44
  20.1 0.7 all-gather.2.cloned.1.call-update
  21.7 94.4 %all-to-all-done = bf16[16,128,1024]{1,2,0:T(8,128)(2,1)} async-done(((bf16[16,128,1024]{1,2,0:T(8,128)(2,1)}), bf16[16,128,1024]{1,2,0:T(8,128)(2,1)}, u32[]{:S(2)}, u32[]{:S(2)}) %all-to-all-start) | async-done | bytes 4194336 | tf_op jit(solution)/shard_map/all_to_all | solution.py:44
  116.1 2.8 copy_bitcast_fusion
  119.3 1.0 fusion
  120.3 1.2 fusion.1
  121.5 1.1 fusion.16
  123.4 8.1 %all-to-all-start.1 = ((bf16[16,16,256]{2,0,1:T(8,128)(2,1)}), bf16[16,16,256]{2,0,1:T(8,128)(2,1)S(1)}, u32[]{:S(2)}, u32[]{:S(2)}) async-start(bf16[16,16,256]{2,0,1:T(8,128)(2,1)} %copy.104), calls=%async_computation.1 | async-start | bytes 262144 | tf_op jit(solution)/shard_map/all_to_all | solution.py:76
  131.5 7.8 %all-to-all-done.1 = bf16[16,16,256]{2,0,1:T(8,128)(2,1)S(1)} async-done(((bf16[16,16,256]{2,0,1:T(8,128)(2,1)}), bf16[16,16,256]{2,0,1:T(8,128)(2,1)S(1)}, u32[]{:S(2)}, u32[]{:S(2)}) %all-to-all-start.1) | async-done | bytes 131104 | tf_op jit(solution)/shard_map/all_to_all | solution.py:76
  139.4 2.7 convolution_convert_fusion.1
  143.2 70.4 %reduce-scatter.2.cloned.1.call-done = bf16[16,2048]{1,0:T(8,128)(2,1)} async-done(((bf16[256,2048]{1,0:T(8,128)(2,1)}), bf16[16,2048]{1,0:T(8,128)(2,1)}) %reduce-scatter.2.cloned.1.call-update) | async-done | bytes 65552 | tf_op jit(solution)/shard_map/reduce_scatter | solution.py:78
  213.6 1.0 fusion.23
  214.6 1.3 convolution_convert_fusion.2
  215.9 1.5 reshape.153
  217.4 38.2 %all_to_all.41 = bf16[32,4,2,2048]{3,2,1,0:T(2,128)(2,1)S(1)} all-to-all(bf16[32,4,2,2048]{3,2,1,0:T(2,128)(2,1)} %reshape.153), channel_id=1, replica_groups=mesh['req'=32,'seq'=16] {'req'}, dimensions={0} | all-to-all | bytes 2097152 | tf_op jit(solution)/shard_map/all_to_all | solution.py:112
  255.6 0.8 copy.109
  256.4 5.4 broadcast_in_dim.64
  261.8 98.5 %all_to_all.42 = bf16[32,16,1,2,2048]{4,3,0,2,1:T(2,128)(2,1)S(1)} all-to-all(bf16[32,16,1,2,2048]{4,3,0,2,1:T(2,128)(2,1)} %bitcast.86), channel_id=1, replica_groups=mesh['req'=32,'seq'=16] {'seq'}, dimensions={1} | all-to-all | bytes 8388608 | tf_op jit(solution)/shard_map/all_to_all | solution.py:116
  360.3 6.5 %copy.110 = bf16[32,16,1,2,2048]{4,3,1,0,2:T(2,128)(2,1)} copy(bf16[32,16,1,2,2048]{4,3,0,2,1:T(2,128)(2,1)S(1)} %all_to_all.42) | data formatting | bytes 8388608 | tf_op jit(solution)/shard_map/all_to_all | solution.py:116
  366.8 7.2 %reshape_squeeze.8 = bf16[1024,2048]{1,0:T(8,128)(2,1)} reshape(bf16[32,16,1,2,2048]{4,3,1,0,2:T(2,128)(2,1)} %copy.110) | data formatting | bytes 8388608 | tf_op jit(solution)/shard_map/reshape;squeeze | solution.py:123
  374.0 4.1 fusion.8
  378.1 3.2 convolution_convert_fusion
  381.3 7.6 %stack_reshape.3 = bf16[32,16,1,2,2048]{4,3,1,0,2:T(2,128)(2,1)} reshape(bf16[1024,2048]{1,0:T(8,128)(2,1)} %convolution_convert_fusion) | data formatting | bytes 8388608 | tf_op jit(solution)/shard_map/stack;reshape | solution.py:128
  389.0 6.0 %copy.111 = bf16[32,16,1,2,2048]{4,3,0,2,1:T(2,128)(2,1)S(1)} copy(bf16[32,16,1,2,2048]{4,3,1,0,2:T(2,128)(2,1)} %stack_reshape.3) | data formatting | bytes 8388608 | tf_op jit(solution)/shard_map/stack;reshape | solution.py:128
  395.0 97.5 %all_to_all.43 = bf16[32,16,1,2,2048]{4,3,0,2,1:T(2,128)(2,1)} all-to-all(bf16[32,16,1,2,2048]{4,3,0,2,1:T(2,128)(2,1)S(1)} %copy.111), channel_id=1, replica_groups=mesh['req'=32,'seq'=16] {'seq'}, dimensions={1} | all-to-all | bytes 8388608 | tf_op jit(solution)/shard_map/all_to_all | solution.py:129
  492.5 7.2 %bitcast_reduce_fusion = bf16[32,4,2,2048]{3,2,0,1:T(2,128)(2,1)S(1)} fusion(bf16[32,4,4,2,2048]{4,3,0,2,1:T(2,128)(2,1)} %bitcast.87), kind=kLoop, calls=%fused_computation.1 | loop fusion | flops 1572864 | bytes 5242880 | tf_op jit(solution)/shard_map/reduce_sum | solution.py:134
  499.7 1.1 copy.112
  500.8 36.4 %all_to_all.44 = bf16[32,4,2,2048]{3,2,1,0:T(2,128)(2,1)} all-to-all(bf16[32,4,2,2048]{3,2,1,0:T(2,128)(2,1)S(1)} %copy.112), channel_id=1, replica_groups=mesh['req'=32,'seq'=16] {'req'}, dimensions={0} | all-to-all | bytes 2097152 | tf_op jit(solution)/shard_map/all_to_all | solution.py:133
  537.2 1.5 reshape.156
  538.7 1.2 fusion.4
  (43 shorter events, 2.7 us)
Async XLA Ops:
  6.5 367.4 %copy-start = (bf16[1,2048,384]{2,1,0:T(8,128)(2,1)S(1)}, bf16[1,2048,384]{2,1,0:T(8,128)(2,1)}, u32[]{:S(2)}) copy-start(bf16[1,2048,384]{2,1,0:T(8,128)(2,1)} %param.20) | copy-start | bytes 4718596
  10.6 10.9 %copy-start.3 = (bf16[1,16,4096]{2,1,0:T(8,128)(2,1)S(1)}, bf16[1,16,4096]{2,1,0:T(8,128)(2,1)}, u32[]{:S(2)}) copy-start(bf16[1,16,4096]{2,1,0:T(8,128)(2,1)} %param.12) | copy-start | bytes 393220
  10.6 105.5 %all-to-all-start = ((bf16[16,128,1024]{1,2,0:T(8,128)(2,1)}), bf16[16,128,1024]{1,2,0:T(8,128)(2,1)}, u32[]{:S(2)}, u32[]{:S(2)}) async-start(bf16[16,128,1024]{1,2,0:T(8,128)(2,1)} %stack.2), calls=%async_computation | async-start | bytes 8388608 | tf_op jit(solution)/shard_map/all_to_all | solution.py:44
  20.1 111.4 %all-gather.2.cloned.1.call-start = ((), (), s32[]{:S(2)}) async-start(), calls=%async_computation.7 | async-start | bytes 1081344 | tf_op jit(solution)/shard_map/all_gather | solution.py:77
  122.6 19.5 %copy-start.4 = (s32[1,16,8]{1,2,0:T(8,128)S(1)}, s32[1,16,8]{1,2,0:T(8,128)}, u32[]{:S(2)}) copy-start(s32[1,16,8]{1,2,0:T(8,128)} %param.18) | copy-start | bytes 1540
  122.6 20.4 %copy-start.6 = (f32[1,16,8]{1,2,0:T(8,128)S(1)}, f32[1,16,8]{1,2,0:T(8,128)}, u32[]{:S(2)}) copy-start(f32[1,16,8]{1,2,0:T(8,128)} %param.19) | copy-start | bytes 1540
  122.6 91.0 %copy-start.1 = (bf16[1,16,2048]{2,1,0:T(8,128)(2,1)S(1)}, bf16[1,16,2048]{2,1,0:T(8,128)(2,1)}, u32[]{:S(2)}) copy-start(bf16[1,16,2048]{2,1,0:T(8,128)(2,1)} %param.11) | copy-start | bytes 196612
  122.6 92.0 %copy-start.5 = (f32[2048]{0:T(1024)S(1)}, f32[2048]{0:T(1024)}, u32[]{:S(2)}) copy-start(f32[2048]{0:T(1024)} %param.17) | copy-start | bytes 24580
  123.4 16.0 %all-to-all-start.1 = ((bf16[16,16,256]{2,0,1:T(8,128)(2,1)}), bf16[16,16,256]{2,0,1:T(8,128)(2,1)S(1)}, u32[]{:S(2)}, u32[]{:S(2)}) async-start(bf16[16,16,256]{2,0,1:T(8,128)(2,1)} %copy.104), calls=%async_computation.1 | async-start | bytes 262144 | tf_op jit(solution)/shard_map/all_to_all | solution.py:76
  131.5 82.1 %reduce-scatter.2.cloned.1.call-start = ((), (), s32[]{:S(2)}) async-start(), calls=%async_computation.8 | async-start | bytes 1114112 | tf_op jit(solution)/shard_map/reduce_scatter | solution.py:78
  374.0 4.1 copy-start.7
  499.7 39.0 %copy-start.2 = (bf16[16,2048]{1,0:T(8,128)(2,1)S(1)}, bf16[16,2048]{1,0:T(8,128)(2,1)}, u32[]{:S(2)}) copy-start(bf16[16,2048]{1,0:T(8,128)(2,1)} %reduce-scatter.2.cloned.1.call-done) | copy-start | bytes 196612
Sparse Core Ops, SparseCore 0:
  24.1 78.9 all-gather.1
  142.2 71.3 reduce-scatter.1
